TPU v7x, 512 devices: a whole 4x4x16 slice. The times are simulated.
512 devices in a mesh: gy: 16 (over x_hi, y, core), gx: 32 (over z, x_lo).
Axes of the slice: x: 4 (x_hi: 2, x_lo: 2; x = x_hi * 2 + x_lo), y: 4, z: 16, core: 2. Of those that a mesh axis runs over, the one named last changes fastest.
Arguments:
- embeddings: bfloat16 [128, 4096, 128], P('gy', 'gx'), may hold values from -180 to 180
- affinity: float32 [4, 128, 4096], P(None, 'gy', 'gx'), may hold values from 0 to 1, as said below
- assignment: int32 [128, 4096], P('gy', 'gx'), may hold values from 0 to 1023
Outputs:
- min_distance: float32 [128, 4096], P('gy', 'gx')
- new_centroids: float32 [1024, 128], replicated
Inputs may be any that keep to these rules, and one draw needn't show every extreme that they name: `affinity`: weight 0 exactly for edges that leave the slab; every other edge weighs 0.05 or more.
All inputs are finite; a program needn't handle non-finite values.
Results may differ from a plain program's by a relative error of at most 0.00045.
Values may be sent and summed in bfloat16 or wider, within the bound.
No kernel may reach another device: no remote copies, remote signals or barrier semaphores. Data moves between devices by JAX's collectives and lax.ppermute only.
A program may use at most 64 MiB of HBM per device.

v0:
```python
import math
import jax
import jax.numpy as jnp
from jax import lax
from jax.sharding import PartitionSpec as P

K = 1024
DEGREE = 4
COEFFS = (0.5, 0.45, 0.35, 0.25, 0.15)


def extended(block, sides, width):
    for axis, dim in sides:
        count = lax.axis_size(axis)
        forward = [(i, i + 1) for i in range(count - 1)]
        backward = [(target, source) for source, target in forward]
        low = lax.ppermute(
            lax.slice_in_dim(block, block.shape[dim] - width, None, axis=dim), axis, forward
        )
        high = lax.ppermute(lax.slice_in_dim(block, 0, width, axis=dim), axis, backward)
        block = jnp.concatenate([low, block, high], axis=dim)
    return block


def degree_of(w_ext):
    w_east, w_south, w_diag, w_anti = (w_ext[0], w_ext[1], w_ext[2], w_ext[3])
    result = w_east[1:-1, 1:-1] + w_east[1:-1, :-2]
    result = result + w_south[1:-1, 1:-1] + w_south[:-2, 1:-1]
    result = result + w_diag[1:-1, 1:-1] + w_diag[:-2, :-2]
    return result + w_anti[1:-1, 1:-1] + w_anti[:-2, 2:]


def edge_sum(w_ext, field):
    w_east, w_south, w_diag, w_anti = (w_ext[0], w_ext[1], w_ext[2], w_ext[3])
    result = w_east[1:-1, 1:-1, None] * field[1:-1, 2:]
    result = result + w_east[1:-1, :-2, None] * field[1:-1, :-2]
    result = result + w_south[1:-1, 1:-1, None] * field[2:, 1:-1]
    result = result + w_south[:-2, 1:-1, None] * field[:-2, 1:-1]
    result = result + w_diag[1:-1, 1:-1, None] * field[2:, 2:]
    result = result + w_diag[:-2, :-2, None] * field[:-2, :-2]
    result = result + w_anti[1:-1, 1:-1, None] * field[2:, :-2]
    return result + w_anti[:-2, 2:, None] * field[:-2, 2:]


def whitening(gram, count):
    lower = jnp.linalg.cholesky(gram)
    identity = jnp.eye(gram.shape[0], dtype=gram.dtype)
    inverse = jax.scipy.linalg.solve_triangular(lower, identity, lower=True)
    return math.sqrt(count) * inverse.T


def on_device(embeddings, affinity, assignment):
    rows, cols, chans = embeddings.shape
    reach_all = DEGREE
    w_width = 1
    w_ext = extended(affinity, (("gy", 1), ("gx", 2)), w_width)
    scale = lax.rsqrt(degree_of(w_ext))[..., None]

    def apply_each(field):
        padded = extended(scale * field, (("gy", 0), ("gx", 1)), 1)
        return scale * edge_sum(w_ext, padded)

    previous = embeddings.astype(jnp.float32)
    current = apply_each(previous)
    filtered = COEFFS[0] * previous + COEFFS[1] * current
    for order in range(2, reach_all + 1):
        following = 2.0 * apply_each(current) - previous
        previous, current = (current, following)
        filtered = filtered + COEFFS[order] * following
    pixels = rows * cols
    flat = filtered.reshape(pixels, chans)
    labels = assignment.reshape(pixels)
    total_pixels = pixels * lax.axis_size("gy") * lax.axis_size("gx")
    clusters = K
    block = 128
    highest = lax.Precision.HIGHEST
    gram_local = lax.dot_general(
        flat, flat, (((0,), (0,)), ((), ())), precision=highest, preferred_element_type=jnp.float32
    )
    gram = lax.psum(gram_local, ("gy", "gx"))
    transform = whitening(gram, total_pixels)
    whitened = jnp.dot(flat, transform, precision=highest, preferred_element_type=jnp.float32)

    def one_block(index):
        first = index * block
        onehot = (labels[:, None] == first + jnp.arange(block, dtype=jnp.int32)[None, :]).astype(
            jnp.float32
        )
        partial_sums = lax.dot_general(
            onehot,
            whitened,
            (((0,), (0,)), ((), ())),
            precision=highest,
            preferred_element_type=jnp.float32,
        )
        return (partial_sums, jnp.sum(onehot, axis=0))

    block_sums, block_counts = lax.map(one_block, jnp.arange(clusters // block, dtype=jnp.int32))
    local_sums = block_sums.reshape(clusters, chans)
    local_counts = block_counts.reshape(clusters)
    sums, counts = lax.psum((local_sums, local_counts), ("gy", "gx"))
    centroids = sums / (counts + 1.0)[:, None]
    norms = jnp.sum(whitened * whitened, axis=1)

    def nearest(index, best):
        centre_part = lax.dynamic_slice_in_dim(centroids, index * block, block, 0)
        cross = lax.dot_general(
            whitened,
            centre_part,
            (((1,), (1,)), ((), ())),
            precision=highest,
            preferred_element_type=jnp.float32,
        )
        part_norms = jnp.sum(centre_part * centre_part, axis=1)
        distance = (norms[:, None] - 2.0 * cross + part_norms[None, :]) / chans
        return jnp.minimum(best, jnp.min(distance, axis=1))

    best = lax.fori_loop(0, clusters // block, nearest, jnp.full((pixels,), jnp.inf, jnp.float32))
    return (best.reshape(rows, cols), centroids)


def solution(mesh):
    return jax.shard_map(
        on_device,
        mesh=mesh,
        in_specs=(P("gy", "gx", None), P(None, "gy", "gx"), P("gy", "gx")),
        out_specs=(P("gy", "gx"), P()),
        check_vma=False,
    )
```

profile of v0, /device:TPU:4, one launch (start us, length us, event | category | flops | bytes accessed | tf_op | source)
XLA Modules:
  0.0 1084.3 jit_solution(14910961055857017236)
XLA Ops:
  7.2 0.8 fusion.72
  8.0 2.0 collective-permute-start
  10.1 7.4 collective-permute-start.1
  17.5 1.3 collective-permute-done.1
  18.8 0.7 pad_maximum_fusion.13
  19.6 3.1 collective-permute-start.2
  22.7 1.3 collective-permute-start.3
  24.2 4.4 collective-permute-done.3
  29.1 1.9 collective-permute-start.4
  31.0 7.3 collective-permute-start.5
  38.3 1.9 collective-permute-done.5
  40.2 1.3 collective-permute-start.6
  41.5 5.4 collective-permute-start.7
  46.9 1.3 collective-permute-done.7
  48.3 1.7 broadcast_multiply_fusion.2
  50.1 1.9 collective-permute-start.8
  52.0 7.3 collective-permute-start.9
  59.3 1.9 collective-permute-done.9
  61.2 1.3 collective-permute-start.10
  62.5 5.4 collective-permute-start.11
  67.9 1.3 collective-permute-done.11
  69.3 1.7 broadcast_multiply_fusion.1
  71.0 1.9 collective-permute-start.12
  73.0 7.3 collective-permute-start.13
  80.2 1.9 collective-permute-done.13
  82.1 1.3 collective-permute-start.14
  83.4 5.7 collective-permute-start.15
  89.2 1.3 collective-permute-done.15
  90.6 1.7 broadcast_multiply_fusion
  92.3 1.9 collective-permute-start.16
  94.3 7.3 collective-permute-start.17
  101.5 1.9 collective-permute-done.17
  103.4 1.3 collective-permute-start.18
  104.7 5.7 collective-permute-start.19
  110.5 1.3 collective-permute-done.19
  111.9 1.7 fusion.14
  113.6 1.6 convolution_bitcast_fusion.1
  115.5 453.4 %all-reduce.3.cloned.1.call-done = f32[128,128]{0,1:T(8,128)} async-done(((f32[128,128]{0,1:T(8,128)}), f32[128,128]{0,1:T(8,128)}) %all-reduce.3.cloned.1.call-update) | async-done | bytes 65552 | tf_op jit(solution)/shard_map/psum | solution.py:80
  568.9 1.0 copy.12
  569.9 11.7 %cholesky.14 = f32[128,128]{1,0:T(8,128)S(1)} custom-call(f32[128,128]{1,0:T(8,128)S(1)} %fusion.63), custom_call_target="Cholesky" | custom-call | tf_op jit(solution)/shard_map/jit(cholesky)/cholesky | solution.py:46
  581.6 0.6 compare_reduce_fusion
  582.3 0.7 fusion.61
  582.9 9.8 custom-call.7
  594.3 23.2 %while.26 = (s32[]{:T(128)}, f32[8,128,128]{2,1,0:T(8,128)}, f32[8,128]{1,0:T(8,128)S(1)}, s32[8,128]{1,0:T(8,128)S(1)}, s32[8]{0:T(128)S(1)}, /*index=5*/f32[10...) while((s32[]{:T(128)}, f32[8,128,128]{2,1,0:T(8,128)}, f32[8,128]{1,0:T(8,128)S(1)}, ...), condition=%wide.region_5.6_spmd, body=%wide.region_3.5_spmd.sunk | while | flops 201850880 | bytes 601725 | solution.py:98
  595.6 1.4 fusion.88
  598.5 1.4 fusion.88
  601.4 1.4 fusion.88
  604.3 1.4 fusion.88
  607.2 1.4 fusion.88
  610.1 1.4 fusion.88
  613.0 1.4 fusion.88
  615.9 1.4 fusion.88
  617.6 101.1 %psum.23 = f32[1024]{0:T(1024)S(1)} all-reduce(f32[1024]{0:T(1024)S(1)} %bitcast.54), channel_id=1, replica_groups=mesh['gy'=16,'gx'=32] {'gy','gx'}, use_global_device_ids=true, to_apply=%region_7.8 | all-reduce | flops 1024 | bytes 8192 | tf_op jit(solution)/shard_map/psum | solution.py:101
  718.7 350.4 %all-reduce.5.cloned.1.call-done = f32[1024,128]{1,0:T(8,128)} async-done(((f32[1024,128]{1,0:T(8,128)}), f32[1024,128]{1,0:T(8,128)}) %all-reduce.5.cloned.1.call-update) | async-done | bytes 524304 | tf_op jit(solution)/shard_map/psum | solution.py:101
  1069.0 1.2 broadcast_divide_fusion
  1070.3 6.3 while.27
  1070.4 0.6 fusion.92
  1071.2 0.6 fusion.92
  1072.0 0.6 fusion.92
  1072.8 0.6 fusion.92
  1073.6 0.6 fusion.92
  1074.4 0.6 fusion.92
  1076.0 0.6 fusion.92
  1076.7 0.8 copy-done.1
  (101 shorter events, 11.4 us)
Async XLA Ops:
  7.2 561.7 %all-reduce.3.cloned.1.call-start = ((), (), s32[]{:S(2)}) async-start(), calls=%async_computation | async-start | bytes 131072 | tf_op jit(solution)/shard_map/psum | solution.py:80
  8.0 20.6 %copy-start.5 = (f32[4,8,128]{2,1,0:T(8,128)S(1)}, f32[4,8,128]{2,1,0:T(8,128)}, u32[]{:S(2)}) copy-start(f32[4,8,128]{2,1,0:T(8,128)} %param.8) | copy-start | bytes 49156
  8.0 9.5 collective-permute-start
  10.1 18.8 %copy-start = (bf16[8,128,128]{2,1,0:T(8,128)(2,1)S(1)}, bf16[8,128,128]{2,1,0:T(8,128)(2,1)}, u32[]{:S(2)}) copy-start(bf16[8,128,128]{2,1,0:T(8,128)(2,1)} %param.7) | copy-start | bytes 786436
  10.1 8.7 collective-permute-start.1
  19.6 4.7 collective-permute-start.2
  22.7 6.0 collective-permute-start.3
  29.1 9.2 collective-permute-start.4
  31.0 9.1 collective-permute-start.5
  40.2 6.8 collective-permute-start.6
  41.5 6.8 collective-permute-start.7
  50.1 9.2 collective-permute-start.8
  52.0 9.1 collective-permute-start.9
  61.2 6.8 collective-permute-start.10
  62.5 6.8 collective-permute-start.11
  71.0 9.2 collective-permute-start.12
  73.0 9.1 collective-permute-start.13
  82.1 7.0 collective-permute-start.14
  83.4 7.0 collective-permute-start.15
  92.3 9.2 collective-permute-start.16
  94.3 9.1 collective-permute-start.17
  103.4 7.0 collective-permute-start.18
  104.7 7.0 collective-permute-start.19
  115.2 953.8 %all-reduce.5.cloned.1.call-start = ((), (), s32[]{:S(2)}) async-start(), calls=%async_computation.1 | async-start | bytes 1048576 | tf_op jit(solution)/shard_map/psum | solution.py:101
  568.8 1.0 copy-start.3
  593.6 0.7 copy-start.2
  1076.6 0.8 copy-start.1
  1076.7 0.8 copy-start.4
Sparse Core Ops, SparseCore 0:
  115.3 453.4 all-reduce.2
  617.7 451.3 all-reduce.4
where the time goes:
time: 1090 us; the launch traced here: 1080 us
  waiting for transfers between devices  823 us (76%)
  blocking collectives  101 us (9%)
  starting transfers between devices  78.3 us (7%)
  other arithmetic  35.1 us (3%)
  matrix products  18.7 us (2%)
  between operations  14.5 us (1%)
    psum x1, waiting for transfers between devices, on_device(): gram = lax.psum(gram_local, ('gy', 'gx'))  453 us
    psum x1, waiting for transfers between devices, on_device(): sums, counts = lax.psum((local_sums, local_counts), ('gy', 'gx'))  350 us
    psum x1, blocking collectives, on_device(): sums, counts = lax.psum((local_sums, local_counts), ('gy', 'gx'))  101 us
    ppermute x10, starting transfers between devices, extended(): lax.ppermute(lax.slice_in_dim(block, 0, width, axis=dim), axis, backward)  42.9 us
    ppermute x10, starting transfers between devices, extended(): lax.ppermute(lax.slice_in_dim(block, block.shape[dim] - width, None, axis...  35.1 us
  transfers between devices with their start and end apart: 22, of which 13 were waited for; matrix products, arithmetic and copies ran while one was open for 0% of the time, Pallas kernels for 0%

commit v1 on v0

--- a/solution.py
+++ b/solution.py
@@ -98,7 +98,7 @@
     block_sums, block_counts = lax.map(one_block, jnp.arange(clusters // block, dtype=jnp.int32))
     local_sums = block_sums.reshape(clusters, chans)
     local_counts = block_counts.reshape(clusters)
-    sums, counts = lax.psum((local_sums, local_counts), ("gy", "gx"))
+    sums, counts = lax.psum(lax.psum((local_sums, local_counts), "gy"), "gx")
     centroids = sums / (counts + 1.0)[:, None]
     norms = jnp.sum(whitened * whitened, axis=1)
 

time: 1090 us -> 1050 us (0.963)
  the two profiles are of different devices: /device:TPU:4 before, /device:TPU:8 now
where the time goes in v1:
time: 1050 us
  waiting for transfers between devices  797 us (76%)
  blocking collectives  101 us (10%)
  starting transfers between devices  64.8 us (6%)
  other arithmetic  35.1 us (3%)
  matrix products  18.7 us (2%)
  between operations  14.2 us (1%)
    psum x1, waiting for transfers between devices, on_device(): gram = lax.psum(gram_local, ('gy', 'gx'))  467 us
    psum x2, waiting for transfers between devices, on_device(): sums, counts = lax.psum(lax.psum((local_sums, local_counts), 'gy'), 'gx')  312 us
    psum x2, blocking collectives, on_device(): sums, counts = lax.psum(lax.psum((local_sums, local_counts), 'gy'), 'gx')  101 us
    ppermute x10, starting transfers between devices, extended(): lax.ppermute(lax.slice_in_dim(block, block.shape[dim] - width, None, axis...  44.7 us
  transfers between devices with their start and end apart: 23, of which 14 were waited for; matrix products, arithmetic and copies ran while one was open for 0% of the time, Pallas kernels for 0%

profile of v1, /device:TPU:8, one launch (start us, length us, event | category | flops | bytes accessed | tf_op | source)
XLA Modules:
  0.0 1045.5 jit_solution(12171578613423203676)
XLA Ops:
  7.2 0.8 fusion.72
  8.0 2.0 collective-permute-start
  10.1 3.8 collective-permute-start.1
  13.9 1.3 collective-permute-done.1
  15.1 0.7 pad_maximum_fusion.13
  15.9 3.4 collective-permute-start.2
  19.3 1.3 collective-permute-start.3
  20.9 4.2 collective-permute-done.3
  25.6 2.3 collective-permute-start.4
  27.9 3.3 collective-permute-start.5
  31.2 1.9 collective-permute-done.5
  33.1 1.3 collective-permute-start.6
  34.4 5.3 collective-permute-start.7
  39.7 1.3 collective-permute-done.7
  41.1 1.7 broadcast_multiply_fusion.2
  42.9 3.0 collective-permute-start.8
  45.9 2.5 collective-permute-start.9
  48.4 1.9 collective-permute-done.9
  50.3 1.3 collective-permute-start.10
  51.6 5.4 collective-permute-start.11
  57.1 1.3 collective-permute-done.11
  58.5 1.7 broadcast_multiply_fusion.1
  60.2 4.6 collective-permute-start.12
  64.8 1.9 collective-permute-start.13
  66.7 1.9 collective-permute-done.13
  68.6 1.3 collective-permute-start.14
  69.9 5.4 collective-permute-start.15
  75.3 1.3 collective-permute-done.15
  76.7 1.7 broadcast_multiply_fusion
  78.5 7.6 collective-permute-start.16
  86.2 1.9 collective-permute-start.17
  88.1 1.9 collective-permute-done.17
  90.0 1.3 collective-permute-start.18
  91.3 5.5 collective-permute-start.19
  96.8 1.3 collective-permute-done.19
  98.2 1.7 fusion.14
  99.9 1.6 convolution_bitcast_fusion.1
  101.8 467.0 %all-reduce.4.cloned.1.call-done = f32[128,128]{0,1:T(8,128)} async-done(((f32[128,128]{0,1:T(8,128)}), f32[128,128]{0,1:T(8,128)}) %all-reduce.4.cloned.1.call-update) | async-done | bytes 65552 | tf_op jit(solution)/shard_map/psum | solution.py:80
  568.9 1.0 copy.12
  569.9 11.7 %cholesky.14 = f32[128,128]{1,0:T(8,128)S(1)} custom-call(f32[128,128]{1,0:T(8,128)S(1)} %fusion.63), custom_call_target="Cholesky" | custom-call | tf_op jit(solution)/shard_map/jit(cholesky)/cholesky | solution.py:46
  581.7 0.6 compare_reduce_fusion
  582.3 0.7 fusion.61
  583.0 9.8 custom-call.7
  594.4 23.2 %while.26 = (s32[]{:T(128)}, f32[8,128,128]{2,1,0:T(8,128)}, f32[8,128]{1,0:T(8,128)S(1)}, s32[8,128]{1,0:T(8,128)S(1)}, s32[8]{0:T(128)S(1)}, /*index=5*/f32[10...) while((s32[]{:T(128)}, f32[8,128,128]{2,1,0:T(8,128)}, f32[8,128]{1,0:T(8,128)S(1)}, ...), condition=%wide.region_5.6_spmd, body=%wide.region_3.5_spmd.sunk | while | flops 201850880 | bytes 601725 | solution.py:98
  595.6 1.4 fusion.88
  598.5 1.4 fusion.88
  601.4 1.4 fusion.88
  604.3 1.4 fusion.88
  607.2 1.4 fusion.88
  610.1 1.4 fusion.88
  613.0 1.4 fusion.88
  615.9 1.4 fusion.88
  617.6 141.8 %all-reduce.6.cloned.1.call-done = f32[1024,128]{1,0:T(8,128)} async-done(((f32[1024,128]{1,0:T(8,128)}), f32[1024,128]{1,0:T(8,128)}) %all-reduce.6.cloned.1.call-update) | async-done | bytes 524304 | tf_op jit(solution)/shard_map/psum | solution.py:101
  759.4 37.0 %psum.38 = f32[1024]{0:T(1024)S(1)} all-reduce(f32[1024]{0:T(1024)S(1)} %bitcast.54), channel_id=1, replica_groups=mesh['gy'=16,'gx'=32] {'gy'}, use_global_device_ids=true, to_apply=%region_8.9 | all-reduce | flops 1024 | bytes 8192 | tf_op jit(solution)/shard_map/psum | solution.py:101
  796.4 64.0 %psum.39 = f32[1024]{0:T(1024)S(1)} all-reduce(f32[1024]{0:T(1024)S(1)} %psum.38), channel_id=1, replica_groups=mesh['gy'=16,'gx'=32] {'gx'}, use_global_device_ids=true, to_apply=%region_9.10 | all-reduce | flops 1024 | bytes 8192 | tf_op jit(solution)/shard_map/psum | solution.py:101
  860.5 170.1 %all-reduce.8.cloned.1.call-done = f32[1024,128]{1,0:T(8,128)} async-done(((f32[1024,128]{1,0:T(8,128)}), f32[1024,128]{1,0:T(8,128)}) %all-reduce.8.cloned.1.call-update) | async-done | bytes 524304 | tf_op jit(solution)/shard_map/psum | solution.py:101
  1030.6 1.2 broadcast_divide_fusion
  1031.8 6.3 while.27
  1032.8 0.6 fusion.92
  1033.6 0.6 fusion.92
  1034.4 0.6 fusion.92
  1035.9 0.6 fusion.92
  1036.7 0.6 fusion.92
  1038.2 0.8 copy-done.1
  (105 shorter events, 12.7 us)
Async XLA Ops:
  7.2 561.7 %all-reduce.4.cloned.1.call-start = ((), (), s32[]{:S(2)}) async-start(), calls=%async_computation | async-start | bytes 131072 | tf_op jit(solution)/shard_map/psum | solution.py:80
  8.0 17.1 %copy-start.5 = (f32[4,8,128]{2,1,0:T(8,128)S(1)}, f32[4,8,128]{2,1,0:T(8,128)}, u32[]{:S(2)}) copy-start(f32[4,8,128]{2,1,0:T(8,128)} %param.8) | copy-start | bytes 49156
  8.0 5.8 collective-permute-start
  10.1 15.3 %copy-start = (bf16[8,128,128]{2,1,0:T(8,128)(2,1)S(1)}, bf16[8,128,128]{2,1,0:T(8,128)(2,1)}, u32[]{:S(2)}) copy-start(bf16[8,128,128]{2,1,0:T(8,128)(2,1)} %param.7) | copy-start | bytes 786436
  10.1 5.1 collective-permute-start.1
  15.9 5.0 collective-permute-start.2
  19.3 5.8 collective-permute-start.3
  25.6 5.6 collective-permute-start.4
  27.9 5.2 collective-permute-start.5
  33.1 6.6 collective-permute-start.6
  34.4 6.7 collective-permute-start.7
  42.9 5.6 collective-permute-start.8
  45.9 4.4 collective-permute-start.9
  50.3 6.8 collective-permute-start.10
  51.6 6.8 collective-permute-start.11
  60.2 6.5 collective-permute-start.12
  64.8 3.8 collective-permute-start.13
  68.6 6.7 collective-permute-start.14
  69.9 6.7 collective-permute-start.15
  78.5 9.6 collective-permute-start.16
  86.2 3.8 collective-permute-start.17
  90.0 6.8 collective-permute-start.18
  91.3 6.8 collective-permute-start.19
  101.6 657.8 %all-reduce.6.cloned.1.call-start = ((), (), s32[]{:S(2)}) async-start(), calls=%async_computation.1 | async-start | bytes 1048576 | tf_op jit(solution)/shard_map/psum | solution.py:101
  568.9 1.0 copy-start.3
  593.7 0.7 copy-start.2
  617.6 413.0 %all-reduce.8.cloned.1.call-start = ((), (), s32[]{:S(2)}) async-start(), calls=%async_computation.2 | async-start | bytes 1048576 | tf_op jit(solution)/shard_map/psum | solution.py:101
  1038.2 0.8 copy-start.1
  1038.2 0.8 copy-start.4
Sparse Core Ops, SparseCore 0:
  101.7 467.1 all-reduce.3
  617.7 141.6 all-reduce.5
  762.3 268.2 all-reduce.7
